TPU v7x, 128 devices: a whole 4x4x4 slice. The times are simulated.
128 devices in a mesh: front: 4 (over x_lo, core), row: 8 (over x_hi, y), col: 4 (over z).
Axes of the slice: x: 4 (x_hi: 2, x_lo: 2; x = x_hi * 2 + x_lo), y: 4, z: 4, core: 2. Of those that a mesh axis runs over, the one named last changes fastest.
Arguments:
- parent_entries: float32 [12288, 12288], P('row', ('front', 'col')), as said below
- child_update: float32 [4, 8192, 8192], P('front', 'row', 'col'), as said below
- child_map: int32 [4, 64], replicated, may hold values from 0 to 95, as said below
- child_mask: int32 [4, 64, 64], P('front'), may hold values from 0 to 1, as said below
Outputs:
- schur: float32 [12288, 12288], P('row', ('front', 'col'))
- panel: float32 [12288, 512], P('row')
Inputs may be any that keep to these rules, and one draw needn't show every extreme that they name: `child_update`: each child's update matrix is symmetric. `parent_entries`: Symmetric. `child_mask`: symmetric in its last two dimensions, ones on the diagonal. Distinct within each child. With v = j mod (16), e = v mod (1), r = (v mod 8) div (1), k = (v div 8) * 1 + e and g = r * 2 + k div (1), child_map[f, j] div (6) equals g.
All inputs are finite; a program needn't handle non-finite values.
Results may differ from a plain program's by a relative error of at most 0.000071.
Values sent between devices are 32-bit elements; how exact they have to be, the bound alone decides.
No kernel may reach another device: no remote copies, remote signals or barrier semaphores. Data moves between devices by JAX's collectives and lax.ppermute only.
A program may use at most 128 MiB of HBM per device.

v0:
```python
import jax
import jax.numpy as jnp
from jax import lax
from jax.sharding import PartitionSpec as P

W = 512
BLK = 128


def broadcast(block, axis, holder):
    block = jnp.where(lax.axis_index(axis) == holder, block, jnp.zeros_like(block))
    return lax.psum(block, axis)


def lookup_table(table, wanted, length):
    positions = jnp.arange(length, dtype=jnp.int32)
    return jnp.sum(jnp.where(wanted[..., None] == positions, table, 0), axis=-1)


def body(parent_entries, child_update, child_map, child_mask):
    grid_rows = lax.axis_size("row")
    grid_cols = lax.axis_size("col")
    groups = lax.axis_size(("front", "col"))
    row_index = lax.axis_index("row")
    column_index = lax.axis_index("col")
    group_index = lax.axis_index(("front", "col"))
    local = child_update[0]
    row_blocks = local.shape[0] // BLK
    column_blocks = local.shape[1] // BLK
    total_blocks = child_map.shape[1]
    fronts_count = child_map.shape[0]
    span = min(row_blocks, column_blocks)
    share = span // grid_rows
    per_group = column_blocks // groups
    group_ratio = groups // grid_rows
    front_rows = parent_entries.shape[0]
    front_cols = parent_entries.shape[1]
    parent_row_blocks = front_rows // BLK
    parent_col_blocks = front_cols // BLK
    window = lax.dynamic_slice(
        child_mask[0],
        (row_index * row_blocks, column_index * column_blocks),
        (row_blocks, column_blocks),
    )
    window = window.astype(jnp.float32)
    tiles = local.reshape(row_blocks, BLK, column_blocks, BLK) * window[:, None, :, None]
    tiles = tiles.reshape(
        row_blocks // span, grid_rows, share, BLK, column_blocks // span, grid_rows, share, BLK
    )
    tiles = tiles.transpose(1, 0, 2, 3, 5, 4, 6, 7)
    tiles = tiles.reshape(grid_rows, row_blocks // grid_rows, BLK, groups, per_group, BLK)
    moved = lax.all_to_all(tiles, "row", split_axis=0, concat_axis=0, tiled=True)
    arrived = lax.all_to_all(moved, ("front", "col"), split_axis=3, concat_axis=3, tiled=True)
    sources = jnp.arange(groups, dtype=jnp.int32)
    source_front = sources // grid_cols
    source_column = sources % grid_cols
    picker = source_front[:, None] == jnp.arange(fronts_count, dtype=jnp.int32)[None, :]
    map_rows = jnp.sum(jnp.where(picker[:, :, None], child_map[None, :, :], 0), axis=1)
    from_rows = jnp.arange(grid_rows, dtype=jnp.int32)
    steps_rows = jnp.arange(row_blocks // grid_rows, dtype=jnp.int32)
    child_rows = (
        from_rows[:, None] * row_blocks
        + steps_rows[None, :] // share * span
        + row_index * share
        + steps_rows[None, :] % share
    )
    row_slots = (
        lookup_table(map_rows[:, None, None, :], child_rows[None, :, :], total_blocks)
        - row_index * parent_row_blocks
    )
    steps_cols = jnp.arange(per_group, dtype=jnp.int32)
    ranked = group_index % group_ratio * per_group + steps_cols
    within = ranked // share * span + group_index // group_ratio * share + ranked % share
    child_cols = source_column[:, None] * column_blocks + within[None, :]
    col_slots = (
        lookup_table(map_rows[:, None, :], child_cols, total_blocks)
        - group_index * parent_col_blocks
    )
    row_hits = (
        row_slots[None] == jnp.arange(parent_row_blocks, dtype=jnp.int32)[:, None, None, None]
    )
    col_hits = col_slots[None] == jnp.arange(parent_col_blocks, dtype=jnp.int32)[:, None, None]
    placement = (row_hits[:, None, :, :, :, None] & col_hits[None, :, :, None, None, :]).astype(
        jnp.float32
    )
    assembled = jnp.einsum(
        "absrtw,rtxswy->axby", placement, arrived, precision=lax.Precision.HIGHEST
    )
    front = parent_entries + assembled.reshape(front_rows, front_cols)
    corner = broadcast(front[:W, :W], "row", 0)
    factor = jnp.linalg.cholesky(corner)
    solved = jax.scipy.linalg.solve_triangular(factor, front[:, :W].T, lower=True).T
    panel = broadcast(solved, ("front", "col"), 0)
    piece = lax.dynamic_slice_in_dim(panel, group_index % group_ratio * front_cols, front_cols, 0)
    across = broadcast(piece, "row", group_index // group_ratio)
    schur = front - jnp.dot(panel, across.T, precision=lax.Precision.HIGHEST)
    global_rows = row_index * front_rows + jnp.arange(front_rows, dtype=jnp.int32)
    global_cols = group_index * front_cols + jnp.arange(front_cols, dtype=jnp.int32)
    keep = (global_rows[:, None] >= W) & (global_cols[None, :] >= W)
    return (jnp.where(keep, schur, 0.0), panel)


def solution(mesh):
    placed = (P("row", ("front", "col")), P("front", "row", "col"), P(), P("front", None, None))
    return jax.shard_map(
        body,
        mesh=mesh,
        in_specs=placed,
        out_specs=(P("row", ("front", "col")), P("row", None)),
        check_vma=False,
    )
```

profile of v0, /device:TPU:0, one launch (start us, length us, event | category | flops | bytes accessed | tf_op | source)
XLA Modules:
  0.0 771.0 jit_solution(14635907823872398243)
XLA Ops:
  8.1 5.4 copy.106
  13.5 4.6 copy_multiply_fusion
  18.1 102.6 %all_to_all.10 = f32[8,1,128,16,1,128]{5,3,2,4,1,0:T(8,128)S(1)} all-to-all(f32[8,1,128,16,1,128]{5,3,2,4,1,0:T(8,128)S(1)} %bitcast.83), channel_id=1, replica_groups=mesh['front'=4,'row'=8,'col'=4] {'row'}, dimensions={0} | all-to-all | bytes 16777216 | tf_op jit(solution)/shard_map/all_to_all | solution.py:52
  120.7 8.1 %copy.80 = f32[8,1,128,16,1,128]{5,0,2,4,1,3:T(8,128)} copy(f32[8,1,128,16,1,128]{5,3,2,4,1,0:T(8,128)S(1)} %all_to_all.10) | data formatting | bytes 16777216 | tf_op jit(solution)/shard_map/all_to_all | solution.py:52
  128.8 6.9 all-to-all-start.1
  136.6 6.1 copy.84
  142.9 92.9 %all-to-all-done.1 = f32[8,1,128,16,1,128]{5,0,2,4,1,3:T(8,128)} async-done(((f32[8,1,128,16,1,128]{5,0,2,4,1,3:T(8,128)}), f32[8,1,128,16,1,128]{5,0,2,4,1,3:T(8,128)}, u32[]{:S(2)}, u32[]{:S(2)}) %all-to-all-start.1) | async-done | bytes 8388640 | tf_op jit(solution)/shard_map/all_to_all | solution.py:53
  235.8 13.4 %fusion.4 = f32[12,128,6,128]{3,0,2,1:T(8,128)} fusion(f32[8,1,128,16,1,128]{5,0,2,4,1,3:T(8,128)} %all-to-all-done.1, pred[6,16]{1,0:T(8,128)(4,1)S(1)} %iota_compare_fusion.5, pred[12,16,8]{1,0,2:T(8,128)(4,1)S(1)} %iota_compare_fusion.3), kind=kOutput, calls=%fused_computation.11 | convolution fusion | flops 1811948544 | bytes 13108832 | tf_op jit(solution)/shard_map/absrtw,rtxswy->axby/dot_general | solution.py:86
  249.2 6.7 copy.103
  255.9 6.8 bitcast_add_fusion
  268.6 85.6 %all-reduce.5.cloned.1.call-done = f32[512,512]{0,1:T(8,128)} async-done(((f32[512,512]{0,1:T(8,128)}), f32[512,512]{0,1:T(8,128)}) %all-reduce.5.cloned.1.call-update) | async-done | bytes 1048592 | tf_op jit(solution)/shard_map/psum | solution.py:12
  354.2 2.5 copy.86
  359.5 11.7 %cholesky.103 = f32[128,128]{1,0:T(8,128)S(1)} custom-call(f32[128,128]{1,0:T(8,128)S(1)} %cholesky.263), custom_call_target="Cholesky" | custom-call | tf_op jit(solution)/shard_map/jit(cholesky)/cholesky | solution.py:91
  371.8 9.8 %custom-call.31 = f32[1,128,128]{1,2,0:T(8,128)S(1)} custom-call(f32[1,128,128]{2,1,0:T(8,128)S(1)} %get-tuple-element.55), custom_call_target="InvertDiagBlocksLowerTriangular" | custom-call | tf_op jit(solution)/shard_map/jit(cholesky)/cholesky | solution.py:91
  384.8 11.7 %cholesky.215 = f32[128,128]{1,0:T(8,128)S(1)} custom-call(f32[128,128]{1,0:T(8,128)S(1)} %cholesky.267), custom_call_target="Cholesky" | custom-call | tf_op jit(solution)/shard_map/jit(cholesky)/cholesky | solution.py:91
  398.9 10.8 %custom-call.32 = f32[1,128,128]{1,2,0:T(8,128)S(1)} custom-call(f32[1,128,128]{2,1,0:T(8,128)} %get-tuple-element.53), custom_call_target="InvertDiagBlocksLowerTriangular" | custom-call | tf_op jit(solution)/shard_map/jit(cholesky)/cholesky | solution.py:91
  414.5 11.7 %cholesky.236 = f32[128,128]{1,0:T(8,128)S(1)} custom-call(f32[128,128]{1,0:T(8,128)S(1)} %cholesky.272), custom_call_target="Cholesky" | custom-call | tf_op jit(solution)/shard_map/jit(cholesky)/cholesky | solution.py:91
  426.9 9.8 %custom-call.33 = f32[1,128,128]{1,2,0:T(8,128)S(1)} custom-call(f32[1,128,128]{2,1,0:T(8,128)S(1)} %get-tuple-element.51), custom_call_target="InvertDiagBlocksLowerTriangular" | custom-call | tf_op jit(solution)/shard_map/jit(cholesky)/cholesky | solution.py:91
  439.2 11.9 %cholesky.253 = f32[128,128]{1,0:T(8,128)S(1)} custom-call(f32[128,128]{1,0:T(8,128)S(1)} %convolution_subtract_fusion.5), custom_call_target="Cholesky" | custom-call | tf_op jit(solution)/shard_map/jit(cholesky)/cholesky | solution.py:91
  457.0 2.3 select_select_fusion
  459.4 14.5 %while.1 = (s32[]{:T(128)}, f32[512,512]{0,1:T(8,128)}, s32[4,2]{0,1:T(2,128)S(1)}, f32[4,128,128]{2,1,0:T(8,128)}, s32[]{:T(128)}) while((s32[]{:T(128)}, f32[512,512]{0,1:T(8,128)}, s32[4,2]{0,1:T(2,128)S(1)}, f32[4,128,128]{2,1,0:T(8,128)}, s32[]{:T(128)}) %tuple.37), condition=%wide.while_cond, body=%wide.while_body.sunk | while | flops 2 | bytes 393829 | solution.py:92
  460.0 2.2 dynamic-slice.8
  463.7 2.2 dynamic-slice.8
  467.3 2.2 dynamic-slice.8
  473.9 40.1 %custom-call.34 = f32[4,128,128]{1,2,0:T(8,128)S(1)} custom-call(f32[4,128,128]{2,1,0:T(8,128)} %get-tuple-element.9), custom_call_target="InvertDiagBlocksLowerTriangular" | custom-call | tf_op jit(solution)/shard_map/jit(_solve_triangular)/triangular_solve | solution.py:92
  520.2 2.5 convolution_subtract_fusion.1
  525.8 126.3 %all-reduce.7.cloned.1.call-done = f32[1536,512]{0,1:T(8,128)} async-done(((f32[1536,512]{0,1:T(8,128)}), f32[1536,512]{0,1:T(8,128)}) %all-reduce.7.cloned.1.call-update) | async-done | bytes 3145744 | tf_op jit(solution)/shard_map/psum | solution.py:12
  652.1 2.8 dynamic-slice_select_fusion
  655.0 2.4 copy.97
  657.3 89.0 %all-reduce.9.cloned.1.call-done = f32[768,512]{0,1:T(8,128)} async-done(((f32[768,512]{0,1:T(8,128)}), f32[768,512]{0,1:T(8,128)}) %all-reduce.9.cloned.1.call-update) | async-done | bytes 1572880 | tf_op jit(solution)/shard_map/psum | solution.py:12
  746.3 11.6 %subtract_select_fusion = f32[1536,768]{0,1:T(8,128)} fusion(f32[1536,768]{0,1:T(8,128)} %copy-done, f32[1536,512]{0,1:T(8,128)S(1)} %copy-done.1, f32[768,512]{0,1:T(8,128)} %all-reduce.9.cloned.1.call-done, pred[1536]{0:T(1024)(128)(4,1)S(1)} %add_compare_fusion, pred[768]{0:T(1024)(128)(4,1)S(1)} %add_compare_fusion.1), kind=kOutput, calls=%fused_computation.7 | convolution fusion | flops 7251296256 | bytes 14158080 | tf_op jit(solution)/shard_map/dot_general | solution.py:96
  758.0 6.0 copy.96
  (94 shorter events, 45.0 us)
Async XLA Ops:
  128.8 7.2 copy-start.6
  128.8 107.0 %all-to-all-start.1 = ((f32[8,1,128,16,1,128]{5,0,2,4,1,3:T(8,128)}), f32[8,1,128,16,1,128]{5,0,2,4,1,3:T(8,128)}, u32[]{:S(2)}, u32[]{:S(2)}) async-start(f32[8,1,128,16,1,128]{5,0,2,4,1,3:T(8,128)} %copy.80), calls=%async_computation.1 | async-start | bytes 16777216 | tf_op jit(solution)/shard_map/all_to_all | solution.py:53
  135.7 218.5 %all-reduce.5.cloned.1.call-start = ((), (), s32[]{:S(2)}) async-start(), calls=%async_computation.2 | async-start | bytes 2097152 | tf_op jit(solution)/shard_map/psum | solution.py:12
  262.8 2.2 copy-start
  266.0 386.0 %all-reduce.7.cloned.1.call-start = ((), (), s32[]{:S(2)}) async-start(), calls=%async_computation.3 | async-start | bytes 6291456 | tf_op jit(solution)/shard_map/psum | solution.py:12
  358.5 1.0 copy-start.3
  371.2 0.6 copy-start.5
  384.1 0.7 copy-start.4
  412.0 1.0 copy-start.2
  525.5 220.9 %all-reduce.9.cloned.1.call-start = ((), (), s32[]{:S(2)}) async-start(), calls=%async_computation.4 | async-start | bytes 3145728 | tf_op jit(solution)/shard_map/psum | solution.py:12
  652.1 2.9 copy-start.1
Sparse Core Ops, SparseCore 0:
  266.2 87.9 all-reduce.4
  525.6 126.4 all-reduce.6
  655.0 91.2 all-reduce.8
where the time goes:
time: 778 us; the launch traced here: 771 us
  waiting for transfers between devices  394 us (51%)
  other arithmetic  144 us (19%)
  blocking collectives  103 us (13%)
  local copies, waits for them, and re-layouts  63.6 us (8%)
  matrix products  42.2 us (5%)
  between operations  17.1 us (2%)
  starting transfers between devices  7.9 us (1%)
    psum x3, waiting for transfers between devices, broadcast(): return lax.psum(block, axis)  301 us
    all_to_all x1, blocking collectives, body(): lax.all_to_all(tiles, 'row', split_axis=0, concat_axis=0, tiled=True)  103 us
    all_to_all x1, waiting for transfers between devices, body(): lax.all_to_all(moved, ('front', 'col'), split_axis=3, concat_axis=3, tile...  92.9 us
    another operation x15, other arithmetic, body(): factor = jnp.linalg.cholesky(corner)  80.8 us
    another operation x3, other arithmetic, body(): jax.scipy.linalg.solve_triangular(factor, front[:, :W].T, lower=True)  42.5 us
    unnamed x18, local copies, waits for them, and re-layouts  25.2 us
  transfers between devices with their start and end apart: 4, of which 4 were waited for; matrix products, arithmetic and copies ran while one was open for 1% of the time, Pallas kernels for 0%

commit v1 on v0

--- a/solution.py
+++ b/solution.py
@@ -9,7 +9,7 @@
 
 def broadcast(block, axis, holder):
     block = jnp.where(lax.axis_index(axis) == holder, block, jnp.zeros_like(block))
-    return lax.psum(block, axis)
+    return jnp.sum(lax.all_gather(block, axis), axis=0)
 
 
 def lookup_table(table, wanted, length):

time: 778 us -> 1070 us (1.38)
  waiting for transfers between devices: 394 us -> 608 us
  local copies, waits for them, and re-layouts: 63.6 us -> 112 us
  other arithmetic: 144 us -> 171 us
    all_gather x0 -> x3, waiting for transfers between devices: none -> 509 us  [broadcast(): return jnp.sum(lax.all_gather(block, axis), axis=0)]
    psum x3 -> x0, waiting for transfers between devices: 301 us -> none  [broadcast(): return lax.psum(block, axis)]
    unnamed x18 -> x16, local copies, waits for them, and re-layouts: 25.2 us -> 82.2 us
    reduce_sum x0 -> x3, other arithmetic: none -> 31 us  [broadcast(): return jnp.sum(lax.all_gather(block, axis), axis=0)]
where the time goes in v1:
time: 1070 us; the launch traced here: 1060 us
  waiting for transfers between devices  608 us (57%)
  other arithmetic  171 us (16%)
  local copies, waits for them, and re-layouts  112 us (10%)
  blocking collectives  103 us (10%)
  matrix products  46.5 us (4%)
  between operations  17.1 us (2%)
    all_gather x3, waiting for transfers between devices, broadcast(): return jnp.sum(lax.all_gather(block, axis), axis=0)  509 us
    all_to_all x1, blocking collectives, body(): lax.all_to_all(tiles, 'row', split_axis=0, concat_axis=0, tiled=True)  103 us
    all_to_all x1, waiting for transfers between devices, body(): lax.all_to_all(moved, ('front', 'col'), split_axis=3, concat_axis=3, tile...  99 us
    unnamed x16, local copies, waits for them, and re-layouts  82.2 us
    another operation x15, other arithmetic, body(): factor = jnp.linalg.cholesky(corner)  81.5 us
    another operation x3, other arithmetic, body(): jax.scipy.linalg.solve_triangular(factor, front[:, :W].T, lower=True)  42.5 us
    reduce_sum x3, other arithmetic, broadcast(): return jnp.sum(lax.all_gather(block, axis), axis=0)  31 us
  transfers between devices with their start and end apart: 4, of which 4 were waited for; matrix products, arithmetic and copies ran while one was open for 1% of the time, Pallas kernels for 0%

profile of v1, /device:TPU:0, one launch (start us, length us, event | category | flops | bytes accessed | tf_op | source)
XLA Modules:
  0.0 1064.6 jit_solution(16272129379875678813)
XLA Ops:
  8.1 5.4 copy.61
  13.5 4.6 copy_multiply_fusion
  18.1 102.6 %all_to_all.10 = f32[8,1,128,16,1,128]{5,3,2,4,1,0:T(8,128)S(1)} all-to-all(f32[8,1,128,16,1,128]{5,3,2,4,1,0:T(8,128)S(1)} %bitcast.97), channel_id=1, replica_groups=mesh['front'=4,'row'=8,'col'=4] {'row'}, dimensions={0} | all-to-all | bytes 16777216 | tf_op jit(solution)/shard_map/all_to_all | solution.py:52
  120.7 8.1 copy.47
  128.8 6.9 all-to-all-start.1
  136.8 99.0 %all-to-all-done.1 = f32[8,1,128,16,1,128]{5,0,2,4,1,3:T(8,128)} async-done(((f32[8,1,128,16,1,128]{5,0,2,4,1,3:T(8,128)}), f32[8,1,128,16,1,128]{5,0,2,4,1,3:T(8,128)}, u32[]{:S(2)}, u32[]{:S(2)}) %all-to-all-start.1) | async-done | bytes 8388640 | tf_op jit(solution)/shard_map/all_to_all | solution.py:53
  235.8 11.9 %fusion.4 = f32[12,128,6,128]{3,0,2,1:T(8,128)S(1)} fusion(f32[8,1,128,16,1,128]{5,0,2,4,1,3:T(8,128)} %all-to-all-done.1, pred[6,16]{1,0:T(8,128)(4,1)S(1)} %iota_compare_fusion.5, pred[12,16,8]{1,0,2:T(8,128)(4,1)S(1)} %iota_compare_fusion.3), kind=kOutput, calls=%fused_computation.13 | convolution fusion | flops 1811948544 | bytes 13108832 | tf_op jit(solution)/shard_map/absrtw,rtxswy->axby/dot_general | solution.py:86
  249.2 3.8 bitcast_add_fusion
  258.9 105.0 %all-gather.7.cloned.1.call-done = f32[4096,512]{1,0:T(8,128)} async-done(((f32[512,512]{1,0:T(8,128)}), f32[4096,512]{1,0:T(8,128)}) %all-gather.7.cloned.1.call-update) | async-done | bytes 8388624 | tf_op jit(solution)/shard_map/all_gather | solution.py:12
  363.9 5.5 reduce_sum.57
  374.6 11.7 %cholesky.103 = f32[128,128]{1,0:T(8,128)S(1)} custom-call(f32[128,128]{1,0:T(8,128)S(1)} %cholesky.263), custom_call_target="Cholesky" | custom-call | tf_op jit(solution)/shard_map/jit(cholesky)/cholesky | solution.py:91
  387.5 9.8 custom-call.31
  400.5 12.1 %cholesky.215 = f32[128,128]{1,0:T(8,128)S(1)} custom-call(f32[128,128]{1,0:T(8,128)S(1)} %cholesky.267), custom_call_target="Cholesky" | custom-call | tf_op jit(solution)/shard_map/jit(cholesky)/cholesky | solution.py:91
  414.6 9.8 custom-call.32
  426.8 11.7 %cholesky.236 = f32[128,128]{1,0:T(8,128)S(1)} custom-call(f32[128,128]{1,0:T(8,128)S(1)} %cholesky.272), custom_call_target="Cholesky" | custom-call | tf_op jit(solution)/shard_map/jit(cholesky)/cholesky | solution.py:91
  439.8 9.8 custom-call.33
  451.9 11.8 %cholesky.253 = f32[128,128]{1,0:T(8,128)S(1)} custom-call(f32[128,128]{1,0:T(8,128)S(1)} %convolution_subtract_fusion.5), custom_call_target="Cholesky" | custom-call | tf_op jit(solution)/shard_map/jit(cholesky)/cholesky | solution.py:91
  470.0 14.1 %while.1 = (s32[]{:T(128)}, f32[512,512]{1,0:T(8,128)}, s32[4,2]{0,1:T(2,128)S(1)}, f32[4,128,128]{2,1,0:T(8,128)}, s32[]{:T(128)}) while((s32[]{:T(128)}, f32[512,512]{1,0:T(8,128)}, s32[4,2]{0,1:T(2,128)S(1)}, f32[4,128,128]{2,1,0:T(8,128)}, s32[]{:T(128)}) %tuple.35), condition=%wide.while_cond, body=%wide.while_body.sunk | while | flops 2 | bytes 132705 | solution.py:92
  470.7 2.9 bitcast_dynamic-update-slice_fusion.2
  474.2 2.9 bitcast_dynamic-update-slice_fusion.2
  477.8 2.9 bitcast_dynamic-update-slice_fusion.2
  484.1 40.1 %custom-call.34 = f32[4,128,128]{1,2,0:T(8,128)S(1)} custom-call(f32[4,128,128]{2,1,0:T(8,128)} %get-tuple-element.9), custom_call_target="InvertDiagBlocksLowerTriangular" | custom-call | tf_op jit(solution)/shard_map/jit(_solve_triangular)/triangular_solve | solution.py:92
  528.3 3.6 convolution_subtract_fusion
  532.8 5.0 convolution_subtract_fusion.1
  540.7 261.6 %all-gather.9.cloned.1.call-done = f32[24576,512]{0,1:T(8,128)} async-done(((f32[1536,512]{0,1:T(8,128)}), f32[24576,512]{0,1:T(8,128)}) %all-gather.9.cloned.1.call-update) | async-done | bytes 50331664 | tf_op jit(solution)/shard_map/all_gather | solution.py:12
  802.2 53.2 %copy.63 = f32[64,8,16,1536]{3,2,1,0:T(8,128)} copy(f32[64,8,16,1536]{3,1,2,0:T(8,128)} %bitcast.94) | data formatting | bytes 100663296
  855.5 16.8 %bitcast_reduce_fusion = f32[1536,512]{0,1:T(8,128)S(1)} fusion(f32[64,8,16,1536]{3,2,1,0:T(8,128)} %copy.63), kind=kLoop, calls=%fused_computation.2 | loop fusion | flops 11796480 | bytes 53477376 | tf_op jit(solution)/shard_map/reduce_sum | solution.py:12
  875.4 3.6 copy.55
  879.0 142.3 %all-gather.11.cloned.1.call-done = f32[6144,512]{0,1:T(8,128)} async-done(((f32[768,512]{0,1:T(8,128)}), f32[6144,512]{0,1:T(8,128)}) %all-gather.11.cloned.1.call-update) | async-done | bytes 12582928 | tf_op jit(solution)/shard_map/all_gather | solution.py:12
  1021.4 15.0 %copy.64 = f32[64,8,8,768]{3,2,1,0:T(8,128)} copy(f32[64,8,8,768]{3,1,2,0:T(8,128)} %bitcast.100) | data formatting | bytes 25165824
  1036.4 8.7 bitcast_reduce_fusion.1
  1045.1 12.5 %subtract_select_fusion = f32[1536,768]{1,0:T(8,128)} fusion(f32[1536,768]{1,0:T(8,128)S(1)} %bitcast.96, f32[1536,512]{0,1:T(8,128)} %copy-done.1, f32[768,512]{0,1:T(8,128)} %bitcast_reduce_fusion.1, pred[768]{0:T(1024)(128)(4,1)S(1)} %add_compare_fusion.1, pred[1536]{0:T(1024)(128)(4,1)S(1)} %add_compare_fusion), kind=kOutput, calls=%fused_computation.9 | convolution fusion | flops 7251296256 | bytes 14158080 | tf_op jit(solution)/shard_map/dot_general | solution.py:96
  (79 shorter events, 46.8 us)
Async XLA Ops:
  128.8 7.2 copy-start.3
  128.8 107.0 %all-to-all-start.1 = ((f32[8,1,128,16,1,128]{5,0,2,4,1,3:T(8,128)}), f32[8,1,128,16,1,128]{5,0,2,4,1,3:T(8,128)}, u32[]{:S(2)}, u32[]{:S(2)}) async-start(f32[8,1,128,16,1,128]{5,0,2,4,1,3:T(8,128)} %copy.47), calls=%async_computation.1 | async-start | bytes 16777216 | tf_op jit(solution)/shard_map/all_to_all | solution.py:53
  135.7 228.2 %all-gather.7.cloned.1.call-start = ((), (), s32[]{:S(2)}) async-start(), calls=%async_computation.2 | async-start | bytes 9437184 | tf_op jit(solution)/shard_map/all_gather | solution.py:12
  253.1 2.2 copy-start
  256.4 545.8 %all-gather.9.cloned.1.call-start = ((), (), s32[]{:S(2)}) async-start(), calls=%async_computation.3 | async-start | bytes 53477376 | tf_op jit(solution)/shard_map/all_gather | solution.py:12
  373.6 1.0 copy-start.2
  540.6 480.8 %all-gather.11.cloned.1.call-start = ((), (), s32[]{:S(2)}) async-start(), calls=%async_computation.4 | async-start | bytes 14155776 | tf_op jit(solution)/shard_map/all_gather | solution.py:12
  872.3 1.8 copy-start.1
  875.4 169.7 %slice-start = ((s8[4718592]{0:T(1024)(128)(4,1)}), s8[524288]{0:T(1024)(128)(4,1)S(1)}, s32[]{:S(2)}) async-start(s8[4718592]{0:T(1024)(128)(4,1)} %bitcast.95), calls=%async_computation.5 | async-start | bytes 1048576
  1021.4 23.8 %slice-start.1 = ((s8[4718592]{0:T(1024)(128)(4,1)}), s8[4194304]{0:T(1024)(128)(4,1)S(1)}, s32[]{:S(2)}) async-start(s8[4718592]{0:T(1024)(128)(4,1)} %bitcast.95), calls=%async_computation.6 | async-start | bytes 8388608
Sparse Core Ops, SparseCore 0:
  256.5 107.2 all-gather.6
  540.7 261.4 all-gather.8
  875.5 145.7 all-gather.10
